TPU v7x, 256 devices: a whole 4x4x8 slice. The times are simulated.
256 devices in a mesh: state: 8 (over z), tile: 32 (over x, y, core).
Axes of the slice: x: 4, y: 4, z: 8, core: 2. Of those that a mesh axis runs over, the one named last changes fastest.
Arguments:
- bands: bfloat16 [8, 240, 524288], P('state', None, 'tile')
- block_slot: int32 [8, 4096], P('state', 'tile'), may hold values from 0 to 7
- tile_counties: int32 [8, 256], P('state', 'tile'), may hold values from 0 to 383, as said below
- county_place: int32 [8, 384], P('state'), may hold values from 0 to 383, as said below
- label: int32 [8, 384], P('state', 'tile'), may hold values from -200 to 200
- w_first: bfloat16 [64, 240], replicated, may hold values from -0.375 to 0.375
- taps: float32 [3, 64], replicated, may hold values from -2 to 2
- w_second: bfloat16 [128, 64], replicated, may hold values from -0.75 to 0.75
- w_third: bfloat16 [128, 128], replicated, may hold values from -0.5 to 0.5
- w_head: bfloat16 [128], replicated, may hold values from -0.5 to 0.5
Outputs:
- county_mean: float32 [8, 384], P('state', 'tile')
- weight_grads: float32 [40256], replicated
Inputs may be any that keep to these rules, and one draw needn't show every extreme that they name: `county_place`: each row is an ordering of the counties of one state region; the county at place p is owned by tile index p // 12 of that region. `tile_counties`: tile t's list names counties of its own state region owned by tile indices t, t + 1, ..., t + 4 - 1 (mod the tile axis's size); at most 4 entries of a list are owned by one tile index, and exactly 4 by t itself.
All inputs are finite; a program needn't handle non-finite values.
Results may differ from a plain program's by a relative error of at most 0.00064.
Values sent between devices are 32-bit elements; how exact they have to be, the bound alone decides.
No kernel may reach another device: no remote copies, remote signals or barrier semaphores. Data moves between devices by JAX's collectives and lax.ppermute only.
A program may use at most 128 MiB of HBM per device.

v0:
```python
import jax
import jax.numpy as jnp
from jax import lax
from jax.sharding import PartitionSpec as P

MOST = 4
REACH = 4


def from_behind(value, axis, by):
    peers = lax.axis_size(axis)
    return lax.ppermute(value, axis, [(i, (i + by) % peers) for i in range(peers)])


def silu_parts(value):
    sig = jax.nn.sigmoid(value)
    return (value * sig, sig * (1.0 + value * (1.0 - sig)))


def along_rows(field, weights, row_len):
    chans, count = field.shape
    grid = field.reshape(chans, count // row_len, row_len)
    padded = jnp.pad(grid, ((0, 0), (0, 0), (1, 1)))
    out = (
        weights[0][:, None, None] * padded[:, :, :-2]
        + weights[1][:, None, None] * grid
        + weights[2][:, None, None] * padded[:, :, 2:]
    )
    return out.reshape(chans, count)


def tap_grads(field, upstream, row_len):
    chans, count = field.shape
    grid = field.reshape(chans, count // row_len, row_len)
    padded = jnp.pad(grid, ((0, 0), (0, 0), (1, 1)))
    above = upstream.reshape(grid.shape)
    return jnp.stack(
        [
            jnp.sum(above * padded[:, :, :-2], axis=(1, 2)),
            jnp.sum(above * grid, axis=(1, 2)),
            jnp.sum(above * padded[:, :, 2:], axis=(1, 2)),
        ]
    )


def contract_last(left, right):
    return lax.dot_general(
        left, right, (((1,), (1,)), ((), ())), preferred_element_type=jnp.float32
    )


def contract_first(left, right):
    return lax.dot_general(
        left, right, (((0,), (0,)), ((), ())), preferred_element_type=jnp.float32
    )


def forward(pixels, w_first, taps, w_second, w_third, w_head, row_len):
    h_one = jnp.dot(w_first, pixels, preferred_element_type=jnp.float32)
    s_one = along_rows(h_one, taps, row_len)
    a_one = silu_parts(s_one)[0].astype(jnp.bfloat16)
    h_two = jnp.dot(w_second, a_one, preferred_element_type=jnp.float32)
    a_two = silu_parts(h_two)[0].astype(jnp.bfloat16)
    h_three = jnp.dot(w_third, a_two, preferred_element_type=jnp.float32)
    a_three = (silu_parts(h_three)[0] + a_two.astype(jnp.float32)).astype(jnp.bfloat16)
    yhat = jnp.dot(w_head, a_three, preferred_element_type=jnp.float32)
    return (h_one, s_one, a_one, h_two, a_two, h_three, a_three, yhat)


def backward(pixels, saved, taps, w_second, w_third, w_head, cotangent, row_len):
    h_one, s_one, a_one, h_two, a_two, h_three, a_three, yhat = saved
    grad_in = cotangent.astype(jnp.bfloat16)
    d_head = jnp.dot(a_three, grad_in, preferred_element_type=jnp.float32)
    d_a3 = w_head.astype(jnp.float32)[:, None] * grad_in.astype(jnp.float32)[None, :]
    d_h3 = (d_a3 * silu_parts(h_three)[1]).astype(jnp.bfloat16)
    d_third = contract_last(d_h3, a_two)
    d_a2 = contract_first(w_third, d_h3) + d_a3
    d_h2 = (d_a2 * silu_parts(h_two)[1]).astype(jnp.bfloat16)
    d_second = contract_last(d_h2, a_one)
    d_a1 = contract_first(w_second, d_h2)
    d_s1 = d_a1 * silu_parts(s_one)[1]
    d_taps = tap_grads(h_one, d_s1, row_len)
    d_h1 = along_rows(d_s1, jnp.stack([taps[2], taps[1], taps[0]]), row_len).astype(jnp.bfloat16)
    d_first = contract_last(d_h1, pixels)
    return jnp.concatenate(
        [d_first.reshape(-1), d_taps.reshape(-1), d_second.reshape(-1), d_third.reshape(-1), d_head]
    )


def slot_stats(yhat, slots, slot_count):
    blocks = slots.shape[0]
    row_len = yhat.shape[0] // blocks
    member = (slots[None, :] == jnp.arange(slot_count, dtype=jnp.int32)[:, None]).astype(
        jnp.float32
    )
    block_sums = jnp.sum(yhat.reshape(blocks, row_len), axis=1)
    return (
        jnp.sum(member * block_sums[None, :], axis=1),
        jnp.sum(member, axis=1) * row_len,
        member,
    )


def place_of(counties, table):
    hits = counties[:, None] == jnp.arange(table.shape[0], dtype=jnp.int32)[None, :]
    return jnp.sum(jnp.where(hits, table[None, :], 0), axis=1)


def judge(sums, counts, labels, devices):
    denom = jnp.maximum(counts, 1.0)
    mean = sums / denom
    live = (counts > 0.5).astype(jnp.float32)
    target = labels.astype(jnp.float32) * 0.01
    return (mean, live * 2.0 * (mean - target) / (devices * denom))


def pixel_cotangent(member, slot_adjoint, row_len):
    block_adjoint = jnp.sum(member * slot_adjoint[:, None], axis=0)
    return jnp.broadcast_to(block_adjoint[:, None], (block_adjoint.shape[0], row_len)).reshape(-1)


def settle(sums, counts, codes, labels, devices):
    flat_codes = codes.reshape(-1)
    owned = jnp.arange(1, labels.shape[0] + 1, dtype=jnp.int32).astype(jnp.float32)
    hit = (flat_codes[:, None] == owned[None, :]).astype(jnp.float32)
    total = jnp.sum(hit * sums.reshape(-1)[:, None], axis=0)
    number = jnp.sum(hit * counts.reshape(-1)[:, None], axis=0)
    mean, adjoint = judge(total, number, labels, devices)
    back = jnp.sum(hit * adjoint[None, :], axis=1).reshape(codes.shape)
    return (mean, back)


def packed(select, values, rows):
    return jnp.sum(select * values[:, None], axis=0).reshape(rows, -1)


def on_device(
    bands, block_slot, tile_counties, county_place, label, w_first, taps, w_second, w_third, w_head
):
    pixels = bands[0]
    slots = block_slot[0]
    row_len = pixels.shape[1] // slots.shape[0]
    slot_total = tile_counties.shape[1]
    saved = forward(pixels, w_first, taps, w_second, w_third, w_head, row_len)
    slot_sums, slot_counts, member = slot_stats(saved[-1], slots, slot_total)
    table = county_place[0]
    place = place_of(tile_counties[0], table)
    labels_mine = label[0]
    cty_dev = labels_mine.shape[0]
    n_tile = lax.axis_size("tile")
    devices = float(lax.axis_size("state") * n_tile)
    owner = place // cty_dev
    local_code = (place % cty_dev + 1).astype(jnp.float32)
    order = jnp.arange(slot_total, dtype=jnp.int32)
    rank = jnp.sum(
        ((owner[:, None] == owner[None, :]) & (order[None, :] < order[:, None])).astype(jnp.int32),
        axis=1,
    )
    me = lax.axis_index("tile")
    position = (owner - me) % n_tile * MOST + rank
    select = (position[:, None] == jnp.arange(REACH * MOST, dtype=jnp.int32)[None, :]).astype(
        jnp.float32
    )
    out_sums = packed(select, slot_sums, REACH)
    out_counts = packed(select, slot_counts, REACH)
    out_codes = packed(select, local_code, REACH)
    got_sums, got_counts, got_codes = ([], [], [])
    for step in range(REACH):
        if step == 0:
            piece = (out_sums[0], out_counts[0], out_codes[0])
        else:
            piece = from_behind((out_sums[step], out_counts[step], out_codes[step]), "tile", step)
        got_sums.append(piece[0])
        got_counts.append(piece[1])
        got_codes.append(piece[2])
    county_mean, back = settle(
        jnp.stack(got_sums), jnp.stack(got_counts), jnp.stack(got_codes), labels_mine, devices
    )
    rows = []
    for step in range(REACH):
        if step == 0:
            rows.append(back[0])
        else:
            rows.append(from_behind(back[step], "tile", -step))
    returned = jnp.stack(rows).reshape(-1)
    slot_adjoint = jnp.sum(select * returned[None, :], axis=1)
    cotangent = pixel_cotangent(member, slot_adjoint, row_len)
    local_grads = backward(pixels, saved, taps, w_second, w_third, w_head, cotangent, row_len)
    weight_grads = lax.psum(local_grads, ("state", "tile"))
    return (county_mean[None, :], weight_grads)


def solution(mesh):
    in_specs = (
        P("state", None, "tile"),
        P("state", "tile"),
        P("state", "tile"),
        P("state", None),
        P("state", "tile"),
        P(),
        P(),
        P(),
        P(),
        P(),
    )
    out_specs = (P("state", "tile"), P())
    return jax.shard_map(
        on_device, mesh=mesh, in_specs=in_specs, out_specs=out_specs, check_vma=False
    )
```

profile of v0, /device:TPU:1, one launch (start us, length us, event | category | flops | bytes accessed | tf_op | source)
XLA Modules:
  0.0 352.5 jit_solution(9751502985637400692)
XLA Ops:
  7.2 0.0 copy-start
  7.2 0.0 all-reduce.4.cloned.1.call-start
  7.2 0.8 slice_bitcast_fusion.5
  8.0 4.7 %fusion.5 = f32[64,128,128]{2,0,1:T(8,128)S(1)} fusion(bf16[64,240]{1,0:T(8,128)(2,1)} %param.15, bf16[1,240,16384]{2,1,0:T(8,128)(2,1)} %param.10), kind=kOutput, calls=%fused_computation.18 | convolution fusion | flops 503316480 | bytes 12089344 | tf_op jit(solution)/shard_map/dot_general | solution.py:59
  12.8 2.4 fusion.18
  15.2 4.6 %multiply_convert_fusion = (bf16[128,16384]{0,1:T(8,128)(2,1)S(1)}, f32[128,16384]{0,1:T(8,128)}) fusion(bf16[64,16384]{1,0:T(8,128)(2,1)S(1)} %fusion.18, bf16[128,64]{0,1:T(8,128)(2,1)S(1)} %copy-done.12), kind=kOutput, calls=%fused_computation.16 | convolution fusion | flops 278921216 | bytes 14696448 | tf_op jit(solution)/shard_map/dot_general | solution.py:62
  19.8 4.6 %add_convert_fusion = (bf16[128,16384]{0,1:T(8,128)(2,1)S(1)}, f32[128,16384]{0,1:T(8,128)}) fusion(bf16[128,16384]{0,1:T(8,128)(2,1)S(1)} %get-tuple-element.37, bf16[128,128]{1,0:T(8,128)(2,1)S(1)} %copy-done), kind=kOutput, calls=%fused_computation.14 | convolution fusion | flops 551550976 | bytes 16809984 | tf_op jit(solution)/shard_map/dot_general | solution.py:64
  24.5 1.9 copy-done.3
  26.5 1.2 fusion.38
  27.6 0.1 reduce_sum.147
  27.8 0.1 convert_reduce_fusion
  28.0 0.2 select_reduce_fusion
  28.2 0.2 convert_reduce_fusion.1
  28.4 0.1 select_reduce_fusion.3
  28.5 0.1 slice_bitcast_fusion.2
  28.5 2.7 collective-permute-start.3
  31.2 1.3 collective-permute-start.4
  32.5 1.7 collective-permute-start.5
  34.2 0.1 slice_bitcast_fusion.6
  34.3 0.5 collective-permute-start
  34.7 1.3 collective-permute-start.1
  36.1 0.1 slice_bitcast_fusion.1
  36.1 2.1 collective-permute-start.2
  38.3 0.5 collective-permute-start.6
  38.7 0.1 collective-permute-done.5
  38.8 0.8 collective-permute-start.7
  39.6 0.1 mul.245
  39.7 2.2 collective-permute-start.8
  41.9 0.6 collective-permute-done.2
  42.5 0.1 eq.84
  42.6 2.0 collective-permute-done.7
  44.6 1.5 collective-permute-done.8
  46.0 0.1 mul.251
  46.1 0.1 fusion.27
  46.2 0.5 fusion.40
  46.8 0.2 fusion.28
  46.9 0.1 slice_bitcast_fusion
  47.0 0.9 collective-permute-start.9
  47.9 2.0 collective-permute-start.10
  49.9 0.3 collective-permute-start.11
  50.2 0.4 collective-permute-done.10
  50.6 3.8 %collective-permute-done.11 = f32[4]{0:T(128)S(1)} collective-permute-done((f32[4]{0:T(128)S(1)}, f32[4]{0:T(128)S(1)}, u32[]{:S(2)}, u32[]{:S(2)}) %collective-permute-start.11) | collective-permute-done | bytes 48 | tf_op jit(solution)/shard_map/ppermute | solution.py:12
  54.4 0.1 mul.264
  54.5 0.2 select_reduce_fusion.2
  54.7 0.1 select_reduce_fusion.1
  54.8 0.1 broadcast_bitcast_fusion
  54.9 10.0 %fusion.4 = bf16[128,16384]{0,1:T(8,128)(2,1)S(1)} fusion(f32[128,16384]{0,1:T(8,128)} %get-tuple-element.40, f32[16384]{0:T(1024)S(1)} %get-tuple-element.18, f32[128]{0:T(128)S(1)} %convert_element_type.84), kind=kLoop, calls=%fused_computation.13 | loop fusion | flops 20971520 | bytes 12648960 | tf_op jit(solution)/shard_map/convert_element_type | solution.py:75
  64.9 1.4 convolution_bitcast_fusion.4
  66.3 0.8 slice-done.1
  67.1 7.6 %fusion.2 = bf16[128,16384]{0,1:T(8,128)(2,1)S(1)} fusion(bf16[128,16384]{0,1:T(8,128)(2,1)S(1)} %fusion.4, bf16[128,128]{1,0:T(8,128)(2,1)S(1)} %copy-done, f32[128,16384]{0,1:T(8,128)S(1)} %bitcast.178, f32[16384]{0:T(1024)S(1)} %get-tuple-element.18, f32[128]{0:T(128)S(1)} %convert_element_type.84), kind=kOutput, calls=%fused_computation.5 | convolution fusion | flops 559939584 | bytes 16876032 | tf_op jit(solution)/shard_map/dot_general | solution.py:53
  74.7 3.5 fusion.21
  78.1 2.5 multiply_reduce_fusion.2
  80.6 2.5 copy.55
  83.1 1.3 fusion.41
  84.5 0.8 copy-done.4
  85.3 0.7 convolution_bitcast_fusion.5
  86.0 0.1 reshape.183
  86.1 9.2 %fusion.8 = f32[64,240]{1,0:T(8,128)S(1)} fusion(bf16[1,240,16384]{2,1,0:T(8,128)(2,1)} %param.10, f32[64,128,128]{2,0,1:T(8,128)} %bitcast.157, f32[64]{0:T(128)S(1)} %get-tuple-element.14, f32[64]{0:T(128)S(1)} %get-tuple-element.16, f32[64]{0:T(128)S(1)} %get-tuple-element.15), kind=kOutput, calls=%fused_computation.21 | convolution fusion | flops 509607936 | bytes 12120832 | tf_op jit(solution)/shard_map/dot_general | solution.py:47
  95.3 0.1 reshape.182
  95.5 0.1 reshape.184
  95.5 0.8 concatenate.3
  96.3 0.0 all-reduce.4.cloned.1.call-update
  96.3 247.7 %all-reduce.4.cloned.1.call-done = f32[40256]{0:T(1024)} async-done(((f32[40256]{0:T(1024)}), f32[40256]{0:T(1024)}) %all-reduce.4.cloned.1.call-update) | async-done | bytes 161040 | tf_op jit(solution)/shard_map/psum | solution.py:189
  344.0 1.6 copy.57
  (45 shorter events, 0.2 us)
Async XLA Ops:
  7.2 12.7 %copy-start = (bf16[128,128]{1,0:T(8,128)(2,1)S(1)}, bf16[128,128]{1,0:T(8,128)(2,1)}, u32[]{:S(2)}) copy-start(bf16[128,128]{1,0:T(8,128)(2,1)} %param.18) | copy-start | bytes 98308
  7.2 336.8 %all-reduce.4.cloned.1.call-start = ((), (), s32[]{:S(2)}) async-start(), calls=%async_computation | async-start | bytes 327680 | tf_op jit(solution)/shard_map/psum | solution.py:189
  12.8 7.1 %copy-start.1 = (f32[64,128,128]{2,0,1:T(8,128)}, f32[64,128,128]{2,0,1:T(8,128)S(1)}, u32[]{:S(2)}) copy-start(f32[64,128,128]{2,0,1:T(8,128)S(1)} %fusion.5) | copy-start | bytes 12582916
  12.8 2.4 copy-start.12
  19.8 4.6 %copy-start.5 = (bf16[128,16384]{0,1:T(8,128)(2,1)}, bf16[128,16384]{0,1:T(8,128)(2,1)S(1)}, u32[]{:S(2)}) copy-start(bf16[128,16384]{0,1:T(8,128)(2,1)S(1)} %get-tuple-element.37) | copy-start | bytes 12582916
  19.8 6.6 %copy-start.8 = (bf16[128]{0:T(256)(128)(2,1)S(1)}, bf16[128]{0:T(256)(128)(2,1)}, u32[]{:S(2)}) copy-start(bf16[128]{0:T(256)(128)(2,1)} %param.19) | copy-start | bytes 772
  24.5 2.0 copy-start.3
  24.5 3.3 copy-start.11
  24.5 3.4 copy-start.7
  24.5 3.5 copy-start.10
  24.5 21.7 %copy-start.9 = (s32[1,12]{1,0:T(1,128)S(1)}, s32[1,12]{1,0:T(1,128)}, u32[]{:S(2)}) copy-start(s32[1,12]{1,0:T(1,128)} %param.14) | copy-start | bytes 148
  28.5 7.6 %collective-permute-start.3 = (f32[4]{0:T(128)S(1)}, f32[4]{0:T(128)S(1)}, u32[]{:S(2)}, u32[]{:S(2)}) collective-permute-start(f32[4]{0:T(128)S(1)} %get-tuple-element.26), channel_id=1, source_target_pairs={{0,1},{1,2},{2,3},{3,4},{4,5},{5,6},{6,7},{7,8},{8,9},{9,10},{10,1... | collective-permute-start | bytes 56 | tf_op jit(solution)/shard_map/ppermute | solution.py:12
  31.2 7.0 %collective-permute-start.4 = (f32[4]{0:T(128)S(1)}, f32[4]{0:T(128)S(1)}, u32[]{:S(2)}, u32[]{:S(2)}) collective-permute-start(f32[4]{0:T(128)S(1)} %get-tuple-element.25), channel_id=1, source_target_pairs={{0,2},{1,3},{2,4},{3,5},{4,6},{5,7},{6,8},{7,9},{8,10},{9,11},{10,... | collective-permute-start | bytes 56 | tf_op jit(solution)/shard_map/ppermute | solution.py:12
  32.5 6.3 %collective-permute-start.5 = (f32[4]{0:T(128)S(1)}, f32[4]{0:T(128)S(1)}, u32[]{:S(2)}, u32[]{:S(2)}) collective-permute-start(f32[4]{0:T(128)S(1)} %get-tuple-element.24), channel_id=1, source_target_pairs={{0,3},{1,4},{2,5},{3,6},{4,7},{5,8},{6,9},{7,10},{8,11},{9,12},{10... | collective-permute-start | bytes 56 | tf_op jit(solution)/shard_map/ppermute | solution.py:12
  34.3 5.4 %collective-permute-start = (f32[4]{0:T(128)S(1)}, f32[4]{0:T(128)S(1)}, u32[]{:S(2)}, u32[]{:S(2)}) collective-permute-start(f32[4]{0:T(128)S(1)} %get-tuple-element.30), channel_id=1, source_target_pairs={{0,1},{1,2},{2,3},{3,4},{4,5},{5,6},{6,7},{7,8},{8,9},{9,10},{10,1... | collective-permute-start | bytes 56 | tf_op jit(solution)/shard_map/ppermute | solution.py:12
  34.7 7.1 %collective-permute-start.1 = (f32[4]{0:T(128)S(1)}, f32[4]{0:T(128)S(1)}, u32[]{:S(2)}, u32[]{:S(2)}) collective-permute-start(f32[4]{0:T(128)S(1)} %get-tuple-element.29), channel_id=1, source_target_pairs={{0,2},{1,3},{2,4},{3,5},{4,6},{5,7},{6,8},{7,9},{8,10},{9,11},{10,... | collective-permute-start | bytes 56 | tf_op jit(solution)/shard_map/ppermute | solution.py:12
  36.1 6.3 %collective-permute-start.2 = (f32[4]{0:T(128)S(1)}, f32[4]{0:T(128)S(1)}, u32[]{:S(2)}, u32[]{:S(2)}) collective-permute-start(f32[4]{0:T(128)S(1)} %get-tuple-element.28), channel_id=1, source_target_pairs={{0,3},{1,4},{2,5},{3,6},{4,7},{5,8},{6,9},{7,10},{8,11},{9,12},{10... | collective-permute-start | bytes 56 | tf_op jit(solution)/shard_map/ppermute | solution.py:12
  38.3 4.3 %collective-permute-start.6 = (f32[4]{0:T(128)S(1)}, f32[4]{0:T(128)S(1)}, u32[]{:S(2)}, u32[]{:S(2)}) collective-permute-start(f32[4]{0:T(128)S(1)} %get-tuple-element.34), channel_id=1, source_target_pairs={{0,1},{1,2},{2,3},{3,4},{4,5},{5,6},{6,7},{7,8},{8,9},{9,10},{10,1... | collective-permute-start | bytes 56 | tf_op jit(solution)/shard_map/ppermute | solution.py:12
  38.8 5.7 %collective-permute-start.7 = (f32[4]{0:T(128)S(1)}, f32[4]{0:T(128)S(1)}, u32[]{:S(2)}, u32[]{:S(2)}) collective-permute-start(f32[4]{0:T(128)S(1)} %get-tuple-element.33), channel_id=1, source_target_pairs={{0,2},{1,3},{2,4},{3,5},{4,6},{5,7},{6,8},{7,9},{8,10},{9,11},{10,... | collective-permute-start | bytes 56 | tf_op jit(solution)/shard_map/ppermute | solution.py:12
  39.7 6.3 %collective-permute-start.8 = (f32[4]{0:T(128)S(1)}, f32[4]{0:T(128)S(1)}, u32[]{:S(2)}, u32[]{:S(2)}) collective-permute-start(f32[4]{0:T(128)S(1)} %get-tuple-element.32), channel_id=1, source_target_pairs={{0,3},{1,4},{2,5},{3,6},{4,7},{5,8},{6,9},{7,10},{8,11},{9,12},{10... | collective-permute-start | bytes 56 | tf_op jit(solution)/shard_map/ppermute | solution.py:12
  47.0 3.2 collective-permute-start.9
  47.9 2.7 collective-permute-start.10
  49.9 4.5 %collective-permute-start.11 = (f32[4]{0:T(128)S(1)}, f32[4]{0:T(128)S(1)}, u32[]{:S(2)}, u32[]{:S(2)}) collective-permute-start(f32[4]{0:T(128)S(1)} %get-tuple-element.20), channel_id=1, source_target_pairs={{0,29},{1,30},{2,31},{3,0},{4,1},{5,2},{6,3},{7,4},{8,5},{9,6},{10... | collective-permute-start | bytes 56 | tf_op jit(solution)/shard_map/ppermute | solution.py:12
  54.9 10.0 %copy-start.6 = (bf16[128,16384]{0,1:T(8,128)(2,1)S(1)}, bf16[128,16384]{0,1:T(8,128)(2,1)}, u32[]{:S(2)}) copy-start(bf16[128,16384]{0,1:T(8,128)(2,1)} %copy-done.5) | copy-start | bytes 12582916
  54.9 11.4 %slice-start = ((s8[8388608]{0:T(1024)(128)(4,1)}), s8[4194304]{0:T(1024)(128)(4,1)S(1)}, s32[]{:S(2)}) async-start(s8[8388608]{0:T(1024)(128)(4,1)} %bitcast.177), calls=%async_computation.1 | async-start | bytes 8388608
  64.9 2.2 slice-start.1
  67.1 7.6 %copy-start.2 = (f32[64,128,128]{2,0,1:T(8,128)S(1)}, f32[64,128,128]{2,0,1:T(8,128)}, u32[]{:S(2)}) copy-start(f32[64,128,128]{2,0,1:T(8,128)} %copy-done.1) | copy-start | bytes 12582916
  83.1 2.2 copy-start.4
Sparse Core Ops, SparseCore 0:
  96.5 247.5 all-reduce.3
where the time goes:
time: 353 us; the launch traced here: 352 us
  waiting for transfers between devices  256 us (73%)
  matrix products  38.8 us (11%)
  other arithmetic  16.9 us (5%)
  starting transfers between devices  16.2 us (5%)
  between operations  14.3 us (4%)
  local copies, waits for them, and re-layouts  10.2 us (3%)
    psum x1, waiting for transfers between devices, on_device(): weight_grads = lax.psum(local_grads, ('state', 'tile'))  248 us
    ppermute x12, starting transfers between devices, from_behind(): lax.ppermute(value, axis, [(i, (i + by) % peers) for i in range(peers)])  16.2 us
    dot_general x3, matrix products, contract_last(): lax.dot_general(left, right, (((1,), (1,)), ((), ())), preferred_element_...  12 us
    dot_general x2, matrix products, contract_first(): lax.dot_general(left, right, (((0,), (0,)), ((), ())), preferred_element_...  11 us
    convert_element_type x1, other arithmetic, backward(): d_h3 = (d_a3 * silu_parts(h_three)[1]).astype(jnp.bfloat16)  9.98 us
    ppermute x12, waiting for transfers between devices, from_behind(): lax.ppermute(value, axis, [(i, (i + by) % peers) for i in range(peers)])  8.37 us
  transfers between devices with their start and end apart: 13, of which 7 were waited for; matrix products, arithmetic and copies ran while one was open for 0% of the time, Pallas kernels for 0%

commit v1 on v0

--- a/solution.py
+++ b/solution.py
@@ -186,7 +186,7 @@
     slot_adjoint = jnp.sum(select * returned[None, :], axis=1)
     cotangent = pixel_cotangent(member, slot_adjoint, row_len)
     local_grads = backward(pixels, saved, taps, w_second, w_third, w_head, cotangent, row_len)
-    weight_grads = lax.psum(local_grads, ("state", "tile"))
+    weight_grads = lax.psum(lax.psum(local_grads, "state"), "tile")
     return (county_mean[None, :], weight_grads)
 
 

time: 353 us -> 289 us (0.82)
  waiting for transfers between devices: 256 us -> 192 us
    psum x1 -> x2, waiting for transfers between devices: 248 us -> 184 us  [on_device(): weight_grads = lax.psum(lax.psum(local_grads, 'state'), 'tile')]
  transfers between devices with their start and end apart: 13 -> 14, of which waited for: 7 -> 8; matrix products, arithmetic and copies ran while one was open for 0% -> 0% of each run, Pallas kernels for 0% -> 0%
where the time goes in v1:
time: 289 us; the launch traced here: 288 us
  waiting for transfers between devices  192 us (66%)
  matrix products  38.8 us (13%)
  other arithmetic  16.9 us (6%)
  starting transfers between devices  16.3 us (6%)
  between operations  14.3 us (5%)
  local copies, waits for them, and re-layouts  10.2 us (4%)
    psum x2, waiting for transfers between devices, on_device(): weight_grads = lax.psum(lax.psum(local_grads, 'state'), 'tile')  184 us
    ppermute x12, starting transfers between devices, from_behind(): lax.ppermute(value, axis, [(i, (i + by) % peers) for i in range(peers)])  16.2 us
    dot_general x3, matrix products, contract_last(): lax.dot_general(left, right, (((1,), (1,)), ((), ())), preferred_element_...  12 us
    dot_general x2, matrix products, contract_first(): lax.dot_general(left, right, (((0,), (0,)), ((), ())), preferred_element_...  11 us
    convert_element_type x1, other arithmetic, backward(): d_h3 = (d_a3 * silu_parts(h_three)[1]).astype(jnp.bfloat16)  9.98 us
    ppermute x12, waiting for transfers between devices, from_behind(): lax.ppermute(value, axis, [(i, (i + by) % peers) for i in range(peers)])  8.37 us
  transfers between devices with their start and end apart: 14, of which 8 were waited for; matrix products, arithmetic and copies ran while one was open for 0% of the time, Pallas kernels for 0%

profile of v1, /device:TPU:1, one launch (start us, length us, event | category | flops | bytes accessed | tf_op | source)
XLA Modules:
  0.0 288.4 jit_solution(13477728835380295256)
XLA Ops:
  7.2 0.0 all-reduce.5.cloned.1.call-start
  7.2 0.8 slice_bitcast_fusion.5
  8.0 4.7 %fusion.5 = f32[64,128,128]{2,0,1:T(8,128)S(1)} fusion(bf16[64,240]{1,0:T(8,128)(2,1)} %param.15, bf16[1,240,16384]{2,1,0:T(8,128)(2,1)} %param.10), kind=kOutput, calls=%fused_computation.18 | convolution fusion | flops 503316480 | bytes 12089344 | tf_op jit(solution)/shard_map/dot_general | solution.py:59
  12.8 2.4 fusion.18
  15.2 4.6 %multiply_convert_fusion = (bf16[128,16384]{0,1:T(8,128)(2,1)S(1)}, f32[128,16384]{0,1:T(8,128)}) fusion(bf16[64,16384]{1,0:T(8,128)(2,1)S(1)} %fusion.18, bf16[128,64]{0,1:T(8,128)(2,1)S(1)} %copy-done.12), kind=kOutput, calls=%fused_computation.16 | convolution fusion | flops 278921216 | bytes 14696448 | tf_op jit(solution)/shard_map/dot_general | solution.py:62
  19.8 4.6 %add_convert_fusion = (bf16[128,16384]{0,1:T(8,128)(2,1)S(1)}, f32[128,16384]{0,1:T(8,128)}) fusion(bf16[128,16384]{0,1:T(8,128)(2,1)S(1)} %get-tuple-element.37, bf16[128,128]{1,0:T(8,128)(2,1)S(1)} %copy-done), kind=kOutput, calls=%fused_computation.14 | convolution fusion | flops 551550976 | bytes 16809984 | tf_op jit(solution)/shard_map/dot_general | solution.py:64
  24.5 1.9 copy-done.3
  26.5 1.2 fusion.38
  27.6 0.1 reduce_sum.147
  27.8 0.1 convert_reduce_fusion
  28.0 0.2 select_reduce_fusion
  28.2 0.2 convert_reduce_fusion.1
  28.4 0.1 select_reduce_fusion.3
  28.5 0.1 slice_bitcast_fusion.2
  28.5 2.7 collective-permute-start.3
  31.2 1.3 collective-permute-start.4
  32.5 1.7 collective-permute-start.5
  34.2 0.1 slice_bitcast_fusion.6
  34.3 0.5 collective-permute-start
  34.7 1.3 collective-permute-start.1
  36.1 0.1 slice_bitcast_fusion.1
  36.1 2.1 collective-permute-start.2
  38.3 0.5 collective-permute-start.6
  38.7 0.1 collective-permute-done.5
  38.8 0.8 collective-permute-start.7
  39.6 0.1 mul.245
  39.7 2.2 collective-permute-start.8
  41.9 0.6 collective-permute-done.2
  42.5 0.1 eq.84
  42.6 2.0 collective-permute-done.7
  44.6 1.5 collective-permute-done.8
  46.0 0.1 mul.251
  46.1 0.1 fusion.27
  46.2 0.5 fusion.40
  46.8 0.2 fusion.28
  46.9 0.1 slice_bitcast_fusion
  47.0 0.9 collective-permute-start.9
  47.9 2.0 collective-permute-start.10
  49.9 0.3 collective-permute-start.11
  50.2 0.4 collective-permute-done.10
  50.6 3.8 %collective-permute-done.11 = f32[4]{0:T(128)S(1)} collective-permute-done((f32[4]{0:T(128)S(1)}, f32[4]{0:T(128)S(1)}, u32[]{:S(2)}, u32[]{:S(2)}) %collective-permute-start.11) | collective-permute-done | bytes 48 | tf_op jit(solution)/shard_map/ppermute | solution.py:12
  54.4 0.1 mul.264
  54.5 0.2 select_reduce_fusion.2
  54.7 0.1 select_reduce_fusion.1
  54.8 0.1 broadcast_bitcast_fusion
  54.9 10.0 %fusion.4 = bf16[128,16384]{0,1:T(8,128)(2,1)S(1)} fusion(f32[128,16384]{0,1:T(8,128)} %get-tuple-element.40, f32[16384]{0:T(1024)S(1)} %get-tuple-element.18, f32[128]{0:T(128)S(1)} %convert_element_type.84), kind=kLoop, calls=%fused_computation.13 | loop fusion | flops 20971520 | bytes 12648960 | tf_op jit(solution)/shard_map/convert_element_type | solution.py:75
  64.9 1.4 convolution_bitcast_fusion.4
  66.3 0.8 slice-done.1
  67.1 7.6 %fusion.2 = bf16[128,16384]{0,1:T(8,128)(2,1)S(1)} fusion(bf16[128,16384]{0,1:T(8,128)(2,1)S(1)} %fusion.4, bf16[128,128]{1,0:T(8,128)(2,1)S(1)} %copy-done, f32[128,16384]{0,1:T(8,128)S(1)} %bitcast.178, f32[16384]{0:T(1024)S(1)} %get-tuple-element.18, f32[128]{0:T(128)S(1)} %convert_element_type.84), kind=kOutput, calls=%fused_computation.5 | convolution fusion | flops 559939584 | bytes 16876032 | tf_op jit(solution)/shard_map/dot_general | solution.py:53
  74.7 3.5 %fusion.21 = f32[8,128,8,128]{3,2,1,0:T(8,128)S(1)} fusion(bf16[128,16384]{0,1:T(8,128)(2,1)S(1)} %fusion.2, bf16[128,64]{0,1:T(8,128)(2,1)S(1)} %copy-done.12, f32[64,128,128]{2,0,1:T(8,128)S(1)} %copy-done.2, f32[64]{0:T(128)S(1)} %get-tuple-element.15, f32[64]{0:T(128)S(1)} %get-tuple-element.16, f32[64]{0:T(128)S(1)} %get-tuple-element.14), kind=kOutput, calls=%fused_computation.43 | convolution fusion | flops 282066944 | bytes 12600064 | tf_op jit(solution)/shard_map/dot_general | solution.py:53
  78.1 2.5 multiply_reduce_fusion.2
  80.6 2.5 copy.55
  83.1 1.3 fusion.41
  84.5 0.8 copy-done.4
  85.3 0.7 convolution_bitcast_fusion.5
  86.0 0.1 reshape.183
  86.1 9.2 %fusion.8 = f32[64,240]{1,0:T(8,128)S(1)} fusion(bf16[1,240,16384]{2,1,0:T(8,128)(2,1)} %param.10, f32[64,128,128]{2,0,1:T(8,128)} %bitcast.157, f32[64]{0:T(128)S(1)} %get-tuple-element.14, f32[64]{0:T(128)S(1)} %get-tuple-element.16, f32[64]{0:T(128)S(1)} %get-tuple-element.15), kind=kOutput, calls=%fused_computation.21 | convolution fusion | flops 509607936 | bytes 12120832 | tf_op jit(solution)/shard_map/dot_general | solution.py:47
  95.3 0.1 reshape.182
  95.5 0.1 reshape.184
  95.5 0.8 concatenate.3
  96.3 0.0 all-reduce.7.cloned.1.call-start
  96.4 67.1 %all-reduce.5.cloned.1.call-done = f32[40256]{0:T(1024)} async-done(((f32[40256]{0:T(1024)}), f32[40256]{0:T(1024)}) %all-reduce.5.cloned.1.call-update) | async-done | bytes 161040 | tf_op jit(solution)/shard_map/psum | solution.py:189
  163.5 116.5 %all-reduce.7.cloned.1.call-done = f32[40256]{0:T(1024)} async-done(((f32[40256]{0:T(1024)}), f32[40256]{0:T(1024)}) %all-reduce.7.cloned.1.call-update) | async-done | bytes 161040 | tf_op jit(solution)/shard_map/psum | solution.py:189
  280.0 1.6 copy.58
  (48 shorter events, 0.3 us)
Async XLA Ops:
  7.2 12.7 %copy-start = (bf16[128,128]{1,0:T(8,128)(2,1)S(1)}, bf16[128,128]{1,0:T(8,128)(2,1)}, u32[]{:S(2)}) copy-start(bf16[128,128]{1,0:T(8,128)(2,1)} %param.18) | copy-start | bytes 98308
  7.2 156.3 %all-reduce.5.cloned.1.call-start = ((), (), s32[]{:S(2)}) async-start(), calls=%async_computation | async-start | bytes 327680 | tf_op jit(solution)/shard_map/psum | solution.py:189
  12.8 7.1 %copy-start.1 = (f32[64,128,128]{2,0,1:T(8,128)}, f32[64,128,128]{2,0,1:T(8,128)S(1)}, u32[]{:S(2)}) copy-start(f32[64,128,128]{2,0,1:T(8,128)S(1)} %fusion.5) | copy-start | bytes 12582916
  12.8 2.4 copy-start.12
  19.8 4.6 %copy-start.5 = (bf16[128,16384]{0,1:T(8,128)(2,1)}, bf16[128,16384]{0,1:T(8,128)(2,1)S(1)}, u32[]{:S(2)}) copy-start(bf16[128,16384]{0,1:T(8,128)(2,1)S(1)} %get-tuple-element.37) | copy-start | bytes 12582916
  19.8 6.6 %copy-start.8 = (bf16[128]{0:T(256)(128)(2,1)S(1)}, bf16[128]{0:T(256)(128)(2,1)}, u32[]{:S(2)}) copy-start(bf16[128]{0:T(256)(128)(2,1)} %param.19) | copy-start | bytes 772
  24.5 2.0 copy-start.3
  24.5 3.3 %copy-start.11 = (s32[1,128]{1,0:T(1,128)S(1)}, s32[1,128]{1,0:T(1,128)}, u32[]{:S(2)}) copy-start(s32[1,128]{1,0:T(1,128)} %param.11) | copy-start | bytes 1540
  24.5 3.4 %copy-start.7 = (s32[1,384]{1,0:T(1,128)S(1)}, s32[1,384]{1,0:T(1,128)}, u32[]{:S(2)}) copy-start(s32[1,384]{1,0:T(1,128)} %param.13) | copy-start | bytes 4612
  24.5 3.5 %copy-start.10 = (s32[1,8]{1,0:T(1,128)S(1)}, s32[1,8]{1,0:T(1,128)}, u32[]{:S(2)}) copy-start(s32[1,8]{1,0:T(1,128)} %param.12) | copy-start | bytes 100
  24.5 21.7 %copy-start.9 = (s32[1,12]{1,0:T(1,128)S(1)}, s32[1,12]{1,0:T(1,128)}, u32[]{:S(2)}) copy-start(s32[1,12]{1,0:T(1,128)} %param.14) | copy-start | bytes 148
  28.5 7.6 %collective-permute-start.3 = (f32[4]{0:T(128)S(1)}, f32[4]{0:T(128)S(1)}, u32[]{:S(2)}, u32[]{:S(2)}) collective-permute-start(f32[4]{0:T(128)S(1)} %get-tuple-element.26), channel_id=1, source_target_pairs={{0,1},{1,2},{2,3},{3,4},{4,5},{5,6},{6,7},{7,8},{8,9},{9,10},{10,1... | collective-permute-start | bytes 56 | tf_op jit(solution)/shard_map/ppermute | solution.py:12
  31.2 7.0 %collective-permute-start.4 = (f32[4]{0:T(128)S(1)}, f32[4]{0:T(128)S(1)}, u32[]{:S(2)}, u32[]{:S(2)}) collective-permute-start(f32[4]{0:T(128)S(1)} %get-tuple-element.25), channel_id=1, source_target_pairs={{0,2},{1,3},{2,4},{3,5},{4,6},{5,7},{6,8},{7,9},{8,10},{9,11},{10,... | collective-permute-start | bytes 56 | tf_op jit(solution)/shard_map/ppermute | solution.py:12
  32.5 6.3 %collective-permute-start.5 = (f32[4]{0:T(128)S(1)}, f32[4]{0:T(128)S(1)}, u32[]{:S(2)}, u32[]{:S(2)}) collective-permute-start(f32[4]{0:T(128)S(1)} %get-tuple-element.24), channel_id=1, source_target_pairs={{0,3},{1,4},{2,5},{3,6},{4,7},{5,8},{6,9},{7,10},{8,11},{9,12},{10... | collective-permute-start | bytes 56 | tf_op jit(solution)/shard_map/ppermute | solution.py:12
  34.3 5.4 %collective-permute-start = (f32[4]{0:T(128)S(1)}, f32[4]{0:T(128)S(1)}, u32[]{:S(2)}, u32[]{:S(2)}) collective-permute-start(f32[4]{0:T(128)S(1)} %get-tuple-element.30), channel_id=1, source_target_pairs={{0,1},{1,2},{2,3},{3,4},{4,5},{5,6},{6,7},{7,8},{8,9},{9,10},{10,1... | collective-permute-start | bytes 56 | tf_op jit(solution)/shard_map/ppermute | solution.py:12
  34.7 7.1 %collective-permute-start.1 = (f32[4]{0:T(128)S(1)}, f32[4]{0:T(128)S(1)}, u32[]{:S(2)}, u32[]{:S(2)}) collective-permute-start(f32[4]{0:T(128)S(1)} %get-tuple-element.29), channel_id=1, source_target_pairs={{0,2},{1,3},{2,4},{3,5},{4,6},{5,7},{6,8},{7,9},{8,10},{9,11},{10,... | collective-permute-start | bytes 56 | tf_op jit(solution)/shard_map/ppermute | solution.py:12
  36.1 6.3 %collective-permute-start.2 = (f32[4]{0:T(128)S(1)}, f32[4]{0:T(128)S(1)}, u32[]{:S(2)}, u32[]{:S(2)}) collective-permute-start(f32[4]{0:T(128)S(1)} %get-tuple-element.28), channel_id=1, source_target_pairs={{0,3},{1,4},{2,5},{3,6},{4,7},{5,8},{6,9},{7,10},{8,11},{9,12},{10... | collective-permute-start | bytes 56 | tf_op jit(solution)/shard_map/ppermute | solution.py:12
  38.3 4.3 %collective-permute-start.6 = (f32[4]{0:T(128)S(1)}, f32[4]{0:T(128)S(1)}, u32[]{:S(2)}, u32[]{:S(2)}) collective-permute-start(f32[4]{0:T(128)S(1)} %get-tuple-element.34), channel_id=1, source_target_pairs={{0,1},{1,2},{2,3},{3,4},{4,5},{5,6},{6,7},{7,8},{8,9},{9,10},{10,1... | collective-permute-start | bytes 56 | tf_op jit(solution)/shard_map/ppermute | solution.py:12
  38.8 5.7 %collective-permute-start.7 = (f32[4]{0:T(128)S(1)}, f32[4]{0:T(128)S(1)}, u32[]{:S(2)}, u32[]{:S(2)}) collective-permute-start(f32[4]{0:T(128)S(1)} %get-tuple-element.33), channel_id=1, source_target_pairs={{0,2},{1,3},{2,4},{3,5},{4,6},{5,7},{6,8},{7,9},{8,10},{9,11},{10,... | collective-permute-start | bytes 56 | tf_op jit(solution)/shard_map/ppermute | solution.py:12
  39.7 6.3 %collective-permute-start.8 = (f32[4]{0:T(128)S(1)}, f32[4]{0:T(128)S(1)}, u32[]{:S(2)}, u32[]{:S(2)}) collective-permute-start(f32[4]{0:T(128)S(1)} %get-tuple-element.32), channel_id=1, source_target_pairs={{0,3},{1,4},{2,5},{3,6},{4,7},{5,8},{6,9},{7,10},{8,11},{9,12},{10... | collective-permute-start | bytes 56 | tf_op jit(solution)/shard_map/ppermute | solution.py:12
  47.0 3.2 %collective-permute-start.9 = (f32[4]{0:T(128)S(1)}, f32[4]{0:T(128)S(1)}, u32[]{:S(2)}, u32[]{:S(2)}) collective-permute-start(f32[4]{0:T(128)S(1)} %get-tuple-element.22), channel_id=1, source_target_pairs={{0,31},{1,0},{2,1},{3,2},{4,3},{5,4},{6,5},{7,6},{8,7},{9,8},{10,9... | collective-permute-start | bytes 56 | tf_op jit(solution)/shard_map/ppermute | solution.py:12
  47.9 2.7 collective-permute-start.10
  49.9 4.5 %collective-permute-start.11 = (f32[4]{0:T(128)S(1)}, f32[4]{0:T(128)S(1)}, u32[]{:S(2)}, u32[]{:S(2)}) collective-permute-start(f32[4]{0:T(128)S(1)} %get-tuple-element.20), channel_id=1, source_target_pairs={{0,29},{1,30},{2,31},{3,0},{4,1},{5,2},{6,3},{7,4},{8,5},{9,6},{10... | collective-permute-start | bytes 56 | tf_op jit(solution)/shard_map/ppermute | solution.py:12
  54.9 10.0 %copy-start.6 = (bf16[128,16384]{0,1:T(8,128)(2,1)S(1)}, bf16[128,16384]{0,1:T(8,128)(2,1)}, u32[]{:S(2)}) copy-start(bf16[128,16384]{0,1:T(8,128)(2,1)} %copy-done.5) | copy-start | bytes 12582916
  54.9 11.4 %slice-start = ((s8[8388608]{0:T(1024)(128)(4,1)}), s8[4194304]{0:T(1024)(128)(4,1)S(1)}, s32[]{:S(2)}) async-start(s8[8388608]{0:T(1024)(128)(4,1)} %bitcast.177), calls=%async_computation.2 | async-start | bytes 8388608
  64.9 2.2 slice-start.1
  67.1 7.6 %copy-start.2 = (f32[64,128,128]{2,0,1:T(8,128)S(1)}, f32[64,128,128]{2,0,1:T(8,128)}, u32[]{:S(2)}) copy-start(f32[64,128,128]{2,0,1:T(8,128)} %copy-done.1) | copy-start | bytes 12582916
  83.1 2.2 copy-start.4
  96.3 183.7 %all-reduce.7.cloned.1.call-start = ((), (), s32[]{:S(2)}) async-start(), calls=%async_computation.1 | async-start | bytes 327680 | tf_op jit(solution)/shard_map/psum | solution.py:189
Sparse Core Ops, SparseCore 0:
  96.5 67.0 all-reduce.4
  166.8 113.1 all-reduce.6
